TPU v7x, 256 devices: a whole 4x4x8 slice. The times are simulated.
256 devices in a mesh: row: 32 (over z_lo, y, core), col: 8 (over z_hi, x).
Axes of the slice: x: 4, y: 4, z: 8 (z_hi: 2, z_lo: 4; z = z_hi * 4 + z_lo), core: 2. Of those that a mesh axis runs over, the one named last changes fastest.
Arguments:
- weights: bfloat16 [8192, 32768], P('row', 'col'), may hold values from -6 to 6
- panel_first: float32 [256, 32768], P('row', 'col'), may hold values from -1 to 2, as said below
- panel_second: float32 [256, 32768], P('row', 'col'), may hold values from -1 to 2, as said below
- removed_first: int32 [512], P('col'), may hold values from -1 to 4095, as said below
- removed_second: int32 [512], P('col'), may hold values from -1 to 4095, as said below
Outputs:
- pruned: bfloat16 [8192, 32768], P('row', 'col')
Inputs may be any that keep to these rules, and one draw needn't show every extreme that they name: `removed_first`: in each list every owner's live slots come first; there are 256 live slots in all, at most 64 for one owner and exactly 64 for some owner; live values of one owner are distinct, and the two lists name no column twice. `removed_second`: same form as removed_first, with its own owners. `panel_first`: together with panel_second, its entries at the columns S1 and S2 are the rows of one symmetric positive definite matrix of order 2 * 256. `panel_second`: rows of the same inverse Hessian as panel_first, for the columns S2.
All inputs are finite; a program needn't handle non-finite values.
Results may differ from a plain program's by a relative error of at most 0.001.
Values may be sent and summed in bfloat16 or wider, within the bound.
No kernel may reach another device: no remote copies, remote signals or barrier semaphores. Data moves between devices by JAX's collectives and lax.ppermute only.
A program may use at most 64 MiB of HBM per device.

v0:
```python
import jax
import jax.numpy as jnp
from jax import lax
from jax.sharding import PartitionSpec as P

highest = lax.Precision.HIGHEST


def pick_columns(matrix, chosen):
    present = chosen >= 0
    column = jnp.where(present, chosen, 0)
    taken = jnp.take(matrix, column, axis=1)
    return jnp.where(present[None, :], taken, jnp.zeros((), matrix.dtype))


def compactor(gathered, total):
    present = gathered >= 0
    position = jnp.cumsum(present.astype(jnp.int32)) - 1
    target = jnp.arange(total, dtype=jnp.int32)
    return (present[:, None] & (position[:, None] == target[None, :])).astype(jnp.float32)


def apply_inverse(factor, matrix):
    return jax.scipy.linalg.cho_solve((factor, True), matrix.T).T


def on_device(weights, panel_first, panel_second, removed_first, removed_second):
    panel_rows = panel_first.shape[0]
    slot_count = removed_first.shape[0]
    row_devices = lax.axis_size("row")
    col_devices = lax.axis_size("col")
    order = panel_rows * row_devices
    lists_first, lists_second = (
        lax.all_gather(removed_first, "col", axis=0, tiled=True),
        lax.all_gather(removed_second, "col", axis=0, tiled=True),
    )
    pack_first = compactor(lists_first, order)
    pack_second = compactor(lists_second, order)
    stacked = jnp.stack([panel_first, panel_second])
    chosen = jnp.concatenate([removed_first, removed_second])
    present = chosen >= 0
    column = jnp.where(present, chosen, 0)
    local_entries = jnp.where(present[None, None, :], jnp.take(stacked, column, axis=2), 0.0)
    everyone = lax.all_gather(local_entries[None], ("row", "col"), axis=0, tiled=True)
    everyone = everyone.reshape(row_devices, col_devices, 2, panel_rows, 2, slot_count)
    everyone = jnp.transpose(everyone, (2, 4, 0, 3, 1, 5)).reshape(
        2, 2, order, col_devices * slot_count
    )
    h_first = jnp.dot(everyone[0, 0], pack_first, precision=highest)
    first_at_second = jnp.dot(everyone[0, 1], pack_second, precision=highest)
    second_at_first = jnp.dot(everyone[1, 0], pack_first, precision=highest)
    second_at_second = jnp.dot(everyone[1, 1], pack_second, precision=highest)
    factor_first = jnp.linalg.cholesky(h_first)
    coupling = apply_inverse(factor_first, second_at_first)
    h_second = second_at_second - jnp.dot(coupling, first_at_second, precision=highest)
    factor_second = jnp.linalg.cholesky(h_second)
    first_local = pick_columns(weights, removed_first)
    first_cols = lax.all_gather(first_local, "col", axis=1, tiled=True)
    w_first = jnp.dot(
        first_cols, pack_first.astype(jnp.bfloat16), preferred_element_type=jnp.float32
    )
    coef_first = apply_inverse(factor_first, w_first)
    panel_whole = lax.all_gather(panel_first, "row", axis=0, tiled=True)
    updated = weights.astype(jnp.float32) - jnp.dot(coef_first, panel_whole, precision=highest)
    panel_next = lax.all_gather(panel_second, "row", axis=0, tiled=True) - jnp.dot(
        coupling, panel_whole, precision=highest
    )
    second_local = pick_columns(updated, removed_second)
    second_cols = lax.all_gather(second_local, "col", axis=1, tiled=True)
    w_second = jnp.dot(second_cols, pack_second, precision=highest)
    coef_second = apply_inverse(factor_second, w_second)
    pruned = updated - jnp.dot(coef_second, panel_next, precision=highest)
    return pruned.astype(jnp.bfloat16)


def solution(mesh):
    return jax.shard_map(
        on_device,
        mesh=mesh,
        in_specs=(P("row", "col"), P("row", "col"), P("row", "col"), P("col"), P("col")),
        out_specs=P("row", "col"),
        check_vma=False,
    )
```

profile of v0, /device:TPU:96, one launch (start us, length us, event | category | flops | bytes accessed | tf_op | source)
XLA Modules:
  0.0 969.7 jit_solution(7421695014664704210)
XLA Ops:
  6.6 1.1 pad_maximum_fusion
  7.7 4.4 copy.21
  12.2 2.9 gather_fusion
  15.5 0.7 copy.22
  16.3 0.7 all-gather.6.cloned.1.call-update
  17.0 0.7 all-gather.8.cloned.1.call-update
  17.8 0.6 dynamic-slice.7
  19.5 15.0 %all-reduce.3 = (s32[512]{0:T(512)S(1)}, s32[512]{0:T(512)S(1)}) all-reduce(s32[512]{0:T(512)S(1)} %dynamic-update-slice.10, s32[512]{0:T(512)S(1)} %dynamic-update-slice.11), channel_id=1, replica_groups=mesh['row'=32,'col'=8] {'col'}, use_global_device_ids=true, to_apply=%add.1 | all-reduce | flops 1024 | bytes 8192
  35.7 2.5 copy.25
  38.1 2.5 gather_fusion.1
  40.8 44.2 %all_gather.23 = bf16[256,512]{0,1:T(8,128)(2,1)S(1)} all-gather(bf16[256,64]{0,1:T(8,128)(2,1)S(1)} %select_bitcast_fusion.3), channel_id=1, replica_groups=mesh['row'=32,'col'=8] {'col'}, dimensions={1}, use_global_device_ids=true | all-gather | bytes 294912 | tf_op jit(solution)/shard_map/all_gather | solution.py:58
  85.0 1.1 fusion.14
  86.1 652.6 %all-gather.4.cloned.1.call-done = f32[256,2,8,128]{3,2,1,0:T(8,128)} async-done(((f32[1,2,8,128]{3,2,1,0:T(8,128)}), f32[256,2,8,128]{3,2,1,0:T(8,128)}) %all-gather.4.cloned.1.call-update) | async-done | bytes 2097168 | tf_op jit(solution)/shard_map/all_gather | solution.py:44
  738.7 5.6 reshape.193
  744.3 6.6 copy.33
  750.8 3.6 reshape.194
  755.0 0.6 fusion.2
  755.8 11.7 %cholesky.130 = f32[128,128]{1,0:T(8,128)S(1)} custom-call(f32[128,128]{1,0:T(8,128)S(1)} %cholesky.194), custom_call_target="Cholesky" | custom-call | tf_op jit(solution)/shard_map/jit(cholesky)/cholesky | solution.py:53
  767.6 9.8 %custom-call.16 = f32[1,128,128]{1,2,0:T(8,128)S(1)} custom-call(f32[1,128,128]{2,1,0:T(8,128)S(1)} %get-tuple-element.67), custom_call_target="InvertDiagBlocksLowerTriangular" | custom-call | tf_op jit(solution)/shard_map/jit(cholesky)/cholesky | solution.py:53
  777.9 11.7 %cholesky.147 = f32[128,128]{1,0:T(8,128)S(1)} custom-call(f32[128,128]{1,0:T(8,128)S(1)} %convolution_subtract_fusion.11), custom_call_target="Cholesky" | custom-call | tf_op jit(solution)/shard_map/jit(cholesky)/cholesky | solution.py:53
  789.6 0.7 compare_reduce_fusion.2
  791.6 3.7 while.6
  792.2 1.3 bitcast_dynamic-update-slice_fusion.4
  794.0 1.3 bitcast_dynamic-update-slice_fusion.4
  795.3 19.9 %custom-call.17 = f32[2,128,128]{1,2,0:T(8,128)S(1)} custom-call(f32[2,128,128]{2,1,0:T(8,128)S(1)} %get-tuple-element.27), custom_call_target="InvertDiagBlocksLowerTriangular" | custom-call | tf_op jit(solution)/shard_map/jit(_cho_solve)/triangular_solve | solution.py:24
  817.5 0.8 fusion.3
  818.3 0.6 convolution_subtract_fusion.3
  819.1 0.7 copy-done.3
  819.8 11.7 %cholesky.164 = f32[128,128]{1,0:T(8,128)S(1)} custom-call(f32[128,128]{1,0:T(8,128)S(1)} %cholesky.197), custom_call_target="Cholesky" | custom-call | tf_op jit(solution)/shard_map/jit(cholesky)/cholesky | solution.py:56
  831.6 9.8 %custom-call.19 = f32[1,128,128]{1,2,0:T(8,128)S(1)} custom-call(f32[1,128,128]{2,1,0:T(8,128)S(1)} %get-tuple-element.63), custom_call_target="InvertDiagBlocksLowerTriangular" | custom-call | tf_op jit(solution)/shard_map/jit(cholesky)/cholesky | solution.py:56
  841.4 1.0 constant_dynamic-update-slice_fusion
  842.5 1.1 convolution_subtract_fusion.10
  843.6 12.1 %cholesky.181 = f32[128,128]{1,0:T(8,128)S(1)} custom-call(f32[128,128]{1,0:T(8,128)S(1)} %convolution_subtract_fusion.10), custom_call_target="Cholesky" | custom-call | tf_op jit(solution)/shard_map/jit(cholesky)/cholesky | solution.py:56
  855.7 0.7 compare_reduce_fusion
  856.4 0.6 compare_reduce_fusion.1
  858.2 3.7 while.7
  858.8 1.3 bitcast_dynamic-update-slice_fusion.5
  860.7 1.3 bitcast_dynamic-update-slice_fusion.5
  862.0 19.7 %custom-call.20 = f32[2,128,128]{1,2,0:T(8,128)S(1)} custom-call(f32[2,128,128]{2,1,0:T(8,128)S(1)} %get-tuple-element.29), custom_call_target="InvertDiagBlocksLowerTriangular" | custom-call | tf_op jit(solution)/shard_map/jit(_cho_solve)/triangular_solve | solution.py:24
  881.7 1.2 fusion.39
  882.9 1.2 convolution_subtract_fusion.9
  885.3 8.3 convolution_subtract_fusion.2
  893.5 5.6 copy.29
  899.2 2.8 gather_fusion.2
  902.1 45.2 %all_gather.26 = f32[256,512]{0,1:T(8,128)S(1)} all-gather(f32[256,64]{0,1:T(8,128)S(1)} %select_bitcast_fusion.2), channel_id=1, replica_groups=mesh['row'=32,'col'=8] {'col'}, dimensions={1}, use_global_device_ids=true | all-gather | bytes 589824 | tf_op jit(solution)/shard_map/all_gather | solution.py:69
  947.3 0.8 fusion.9
  949.9 8.0 convolution_subtract_fusion.1
  957.9 5.1 fusion
  (91 shorter events, 11.6 us)
Async XLA Ops:
  6.5 11.2 %copy-start.6 = (u32[256]{0:T(256)S(1)}, u32[256]{0:T(256)}, u32[]{:S(2)}) copy-start(u32[256]{0:T(256)} %constant.149) | copy-start | bytes 3076
  6.5 5.5 copy-start.4
  6.5 5.5 copy-start.5
  6.5 29.1 %copy-start.1 = (bf16[256,4096]{1,0:T(8,128)(2,1)S(1)}, bf16[256,4096]{1,0:T(8,128)(2,1)}, u32[]{:S(2)}) copy-start(bf16[256,4096]{1,0:T(8,128)(2,1)} %param.8) | copy-start | bytes 6291460
  6.5 732.1 %all-gather.4.cloned.1.call-start = ((), (), s32[]{:S(2)}) async-start(), calls=%async_computation | async-start | bytes 2105344 | tf_op jit(solution)/shard_map/all_gather | solution.py:44
  16.2 869.0 %all-gather.6.cloned.1.call-start = ((), (), s32[]{:S(2)}) async-start(), calls=%async_computation.1 | async-start | bytes 4325376 | tf_op jit(solution)/shard_map/all_gather | solution.py:63
  17.0 932.9 %all-gather.8.cloned.1.call-start = ((), (), s32[]{:S(2)}) async-start(), calls=%async_computation.2 | async-start | bytes 4325376 | tf_op jit(solution)/shard_map/all_gather | solution.py:65
  818.3 67.0 %copy-start.2 = (bf16[256,4096]{1,0:T(8,128)(2,1)S(1)}, bf16[256,4096]{1,0:T(8,128)(2,1)}, u32[]{:S(2)}) copy-start(bf16[256,4096]{1,0:T(8,128)(2,1)} %param.8) | copy-start | bytes 6291460
  819.1 0.7 copy-start.3
  949.9 8.0 copy-start
Sparse Core Ops, SparseCore 0:
  16.4 722.2 all-gather.3
  740.5 55.9 all-gather.5
  798.3 62.1 all-gather.7
where the time goes:
time: 977 us; the launch traced here: 970 us
  waiting for transfers between devices  654 us (67%)
  other arithmetic  111 us (11%)
  blocking collectives  104 us (11%)
  local copies, waits for them, and re-layouts  47.1 us (5%)
  matrix products  35.8 us (4%)
  between operations  16.9 us (2%)
    all_gather x1, waiting for transfers between devices, on_device(): lax.all_gather(local_entries[None], ('row', 'col'), axis=0, tiled=True)  653 us
    all_gather x1, blocking collectives, on_device(): second_cols = lax.all_gather(second_local, 'col', axis=1, tiled=True)  45.2 us
    all_gather x1, blocking collectives, on_device(): first_cols = lax.all_gather(first_local, 'col', axis=1, tiled=True)  44.2 us
    another operation x5, other arithmetic, apply_inverse(): return jax.scipy.linalg.cho_solve((factor, True), matrix.T).T  39.6 us
    another operation x7, other arithmetic, on_device(): factor_second = jnp.linalg.cholesky(h_second)  34.9 us
    another operation x6, other arithmetic, on_device(): factor_first = jnp.linalg.cholesky(h_first)  34 us
  transfers between devices with their start and end apart: 3, of which 1 were waited for; matrix products, arithmetic and copies ran while one was open for 18% of the time, Pallas kernels for 0%

commit v1 on v0

--- a/solution.py
+++ b/solution.py
@@ -25,6 +25,13 @@
 
 
 def on_device(weights, panel_first, panel_second, removed_first, removed_second):
+
+    def finish_limits(w_in):
+        val = jnp.stack([w_in for _ in range(lax.axis_size(("row", "col")))], axis=0)
+        state_now = lax.all_to_all(val, concat_axis=0, axis_name=("row", "col"), split_axis=0)
+        then = jnp.concatenate(state_now, axis=0)
+        return then
+
     panel_rows = panel_first.shape[0]
     slot_count = removed_first.shape[0]
     row_devices = lax.axis_size("row")
@@ -41,7 +48,7 @@
     present = chosen >= 0
     column = jnp.where(present, chosen, 0)
     local_entries = jnp.where(present[None, None, :], jnp.take(stacked, column, axis=2), 0.0)
-    everyone = lax.all_gather(local_entries[None], ("row", "col"), axis=0, tiled=True)
+    everyone = finish_limits(local_entries[None])
     everyone = everyone.reshape(row_devices, col_devices, 2, panel_rows, 2, slot_count)
     everyone = jnp.transpose(everyone, (2, 4, 0, 3, 1, 5)).reshape(
         2, 2, order, col_devices * slot_count

time: 977 us -> 390 us (0.40)
  the two profiles are of different devices: /device:TPU:96 before, /device:TPU:6 now
where the time goes in v1:
time: 390 us; the launch traced here: 382 us
  blocking collectives  154 us (39%)
  other arithmetic  111 us (28%)
  local copies, waits for them, and re-layouts  47.7 us (12%)
  matrix products  35.8 us (9%)
  between operations  17.2 us (4%)
  starting transfers between devices  14.7 us (4%)
    unnamed x1, blocking collectives  64.7 us
    all_gather x1, blocking collectives, on_device(): second_cols = lax.all_gather(second_local, 'col', axis=1, tiled=True)  45.1 us
    all_gather x1, blocking collectives, on_device(): first_cols = lax.all_gather(first_local, 'col', axis=1, tiled=True)  44.6 us
    another operation x5, other arithmetic, apply_inverse(): return jax.scipy.linalg.cho_solve((factor, True), matrix.T).T  39.6 us
    another operation x7, other arithmetic, on_device(): factor_second = jnp.linalg.cholesky(h_second)  34.9 us
    another operation x6, other arithmetic, on_device(): factor_first = jnp.linalg.cholesky(h_first)  34 us
    all_to_all x1, starting transfers between devices, finish_limits(): lax.all_to_all(val, concat_axis=0, axis_name=('row', 'col'), split_axis=0)  14.6 us
    dot_general x1, matrix products, on_device(): jnp.dot(coef_first, panel_whole, precision=highest)  8.27 us
  transfers between devices with their start and end apart: 3, of which 0 were waited for; matrix products, arithmetic and copies ran while one was open for 47% of the time, Pallas kernels for 0%

profile of v1, /device:TPU:6, one launch (start us, length us, event | category | flops | bytes accessed | tf_op | source)
XLA Modules:
  0.0 382.5 jit_solution(6752058354706420848)
XLA Ops:
  6.5 0.7 all-gather.3.cloned.1.call-update
  7.3 1.0 pad_maximum_fusion
  8.2 4.4 %copy.31 = f32[2,8,4096]{1,0,2:T(2,128)} copy(f32[2,8,4096]{2,1,0:T(8,128)S(1)} %pad_maximum_fusion) | data formatting | bytes 524288 | tf_op jit(solution)/shard_map/stack | solution.py:46
  12.7 2.9 gather_fusion
  16.1 1.5 stack.15
  17.7 14.6 %all-to-all-start = ((f32[256,1,2,8,128]{4,3,2,1,0:T(8,128)}), f32[256,1,2,8,128]{4,3,2,1,0:T(8,128)S(1)}, u32[]{:S(2)}, u32[]{:S(2)}) async-start(f32[256,1,2,8,128]{4,3,2,1,0:T(8,128)} %stack.15), calls=%async_computation | async-start | bytes 4194304 | tf_op jit(solution)/shard_map/all_to_all | solution.py:31
  32.4 0.7 all-gather.5.cloned.1.call-update
  33.1 0.6 dynamic-slice.7
  34.8 64.7 %all-reduce.3 = (s32[512]{0:T(512)S(1)}, s32[512]{0:T(512)S(1)}) all-reduce(s32[512]{0:T(512)S(1)} %dynamic-update-slice.10, s32[512]{0:T(512)S(1)} %dynamic-update-slice.11), channel_id=1, replica_groups=mesh['row'=32,'col'=8] {'col'}, use_global_device_ids=true, to_apply=%add.1 | all-reduce | flops 1024 | bytes 8192
  100.3 4.1 %copy.35 = bf16[256,4096]{0,1:T(8,128)(2,1)} copy(bf16[256,4096]{1,0:T(8,128)(2,1)} %param.8) | data formatting | bytes 4194304 | tf_op args[0]
  104.4 2.5 gather_fusion.1
  107.3 44.6 %all_gather.19 = bf16[256,512]{0,1:T(8,128)(2,1)S(1)} all-gather(bf16[256,64]{0,1:T(8,128)(2,1)S(1)} %select_bitcast_fusion.4), channel_id=1, replica_groups=mesh['row'=32,'col'=8] {'col'}, dimensions={1}, use_global_device_ids=true | all-gather | bytes 294912 | tf_op jit(solution)/shard_map/all_gather | solution.py:65
  152.0 1.1 fusion.14
  153.2 3.6 reshape_reshape.3
  156.8 6.6 %copy.33 = f32[2,2,32,8,8,64]{5,4,3,2,1,0:T(8,128)} copy(f32[2,2,32,8,8,64]{5,1,3,0,4,2:T(2,128)} %bitcast.130) | data formatting | bytes 4194304 | tf_op jit(solution)/shard_map/transpose | solution.py:53
  163.4 3.6 reshape.187
  167.6 0.6 fusion.2
  168.4 11.7 %cholesky.130 = f32[128,128]{1,0:T(8,128)S(1)} custom-call(f32[128,128]{1,0:T(8,128)S(1)} %cholesky.194), custom_call_target="Cholesky" | custom-call | tf_op jit(solution)/shard_map/jit(cholesky)/cholesky | solution.py:60
  180.1 9.8 %custom-call.16 = f32[1,128,128]{1,2,0:T(8,128)S(1)} custom-call(f32[1,128,128]{2,1,0:T(8,128)S(1)} %get-tuple-element.67), custom_call_target="InvertDiagBlocksLowerTriangular" | custom-call | tf_op jit(solution)/shard_map/jit(cholesky)/cholesky | solution.py:60
  190.4 11.7 %cholesky.147 = f32[128,128]{1,0:T(8,128)S(1)} custom-call(f32[128,128]{1,0:T(8,128)S(1)} %convolution_subtract_fusion.11), custom_call_target="Cholesky" | custom-call | tf_op jit(solution)/shard_map/jit(cholesky)/cholesky | solution.py:60
  202.2 0.7 compare_reduce_fusion.2
  204.2 3.7 while.6
  204.8 1.3 bitcast_dynamic-update-slice_fusion.4
  206.6 1.3 bitcast_dynamic-update-slice_fusion.4
  207.9 19.9 %custom-call.17 = f32[2,128,128]{1,2,0:T(8,128)S(1)} custom-call(f32[2,128,128]{2,1,0:T(8,128)S(1)} %get-tuple-element.27), custom_call_target="InvertDiagBlocksLowerTriangular" | custom-call | tf_op jit(solution)/shard_map/jit(_cho_solve)/triangular_solve | solution.py:24
  230.1 0.8 fusion.3
  230.9 0.6 convolution_subtract_fusion.3
  231.7 0.7 copy-done.2
  232.4 11.7 %cholesky.164 = f32[128,128]{1,0:T(8,128)S(1)} custom-call(f32[128,128]{1,0:T(8,128)S(1)} %cholesky.197), custom_call_target="Cholesky" | custom-call | tf_op jit(solution)/shard_map/jit(cholesky)/cholesky | solution.py:63
  244.2 9.8 %custom-call.19 = f32[1,128,128]{1,2,0:T(8,128)S(1)} custom-call(f32[1,128,128]{2,1,0:T(8,128)S(1)} %get-tuple-element.63), custom_call_target="InvertDiagBlocksLowerTriangular" | custom-call | tf_op jit(solution)/shard_map/jit(cholesky)/cholesky | solution.py:63
  254.0 1.0 constant_dynamic-update-slice_fusion
  255.0 1.1 convolution_subtract_fusion.10
  256.1 12.1 %cholesky.181 = f32[128,128]{1,0:T(8,128)S(1)} custom-call(f32[128,128]{1,0:T(8,128)S(1)} %convolution_subtract_fusion.10), custom_call_target="Cholesky" | custom-call | tf_op jit(solution)/shard_map/jit(cholesky)/cholesky | solution.py:63
  268.3 0.7 compare_reduce_fusion
  268.9 0.6 compare_reduce_fusion.1
  270.8 3.7 while.7
  271.4 1.3 bitcast_dynamic-update-slice_fusion.5
  273.2 1.3 bitcast_dynamic-update-slice_fusion.5
  274.5 19.7 %custom-call.20 = f32[2,128,128]{1,2,0:T(8,128)S(1)} custom-call(f32[2,128,128]{2,1,0:T(8,128)S(1)} %get-tuple-element.29), custom_call_target="InvertDiagBlocksLowerTriangular" | custom-call | tf_op jit(solution)/shard_map/jit(_cho_solve)/triangular_solve | solution.py:24
  294.2 1.2 fusion.39
  295.4 1.2 convolution_subtract_fusion.9
  297.8 8.3 %convolution_subtract_fusion.2 = f32[256,4096]{1,0:T(8,128)} fusion(f32[256,4096]{1,0:T(8,128)} %all-gather.3.cloned.1.call-done, bf16[256,4096]{1,0:T(8,128)(2,1)S(1)} %copy-done.1, f32[128,256]{1,0:T(8,128)S(1)} %fusion.56, f32[128,256]{1,0:T(8,128)S(1)} %fusion.53), kind=kOutput, calls=%fused_computation.9 | convolution fusion | flops 3223388160 | bytes 10747904 | tf_op jit(solution)/shard_map/dot_general | solution.py:71
  306.1 5.6 %copy.39 = f32[256,4096]{0,1:T(8,128)} copy(f32[256,4096]{1,0:T(8,128)} %convolution_subtract_fusion.2) | data formatting | bytes 8388608 | tf_op jit(solution)/shard_map/sub | solution.py:71
  311.7 2.8 gather_fusion.2
  314.7 45.1 %all_gather.22 = f32[256,512]{0,1:T(8,128)S(1)} all-gather(f32[256,64]{0,1:T(8,128)S(1)} %select_bitcast_fusion.3), channel_id=1, replica_groups=mesh['row'=32,'col'=8] {'col'}, dimensions={1}, use_global_device_ids=true | all-gather | bytes 589824 | tf_op jit(solution)/shard_map/all_gather | solution.py:76
  359.8 0.8 fusion.9
  362.4 8.0 %convolution_subtract_fusion.1 = f32[256,4096]{1,0:T(8,128)S(1)} fusion(f32[256,4096]{1,0:T(8,128)} %all-gather.5.cloned.1.call-done, f32[256,4096]{1,0:T(8,128)} %all-gather.3.cloned.1.call-done, f32[128,256]{1,0:T(8,128)S(1)} %fusion.54, f32[128,256]{1,0:T(8,128)S(1)} %fusion.52), kind=kOutput, calls=%fused_computation.8 | convolution fusion | flops 3222339584 | bytes 12845056 | tf_op jit(solution)/shard_map/dot_general | solution.py:72
  370.4 5.1 %fusion = bf16[256,4096]{1,0:T(8,128)(2,1)} fusion(f32[256,4096]{1,0:T(8,128)S(1)} %copy-done, f32[256,4096]{1,0:T(8,128)S(1)} %convolution_subtract_fusion.1, f32[128,256]{1,0:T(8,128)S(1)} %fusion.48, f32[128,256]{1,0:T(8,128)S(1)} %fusion.47), kind=kOutput, calls=%fused_computation.10 | convolution fusion | flops 3223388160 | bytes 10747904 | tf_op jit(solution)/shard_map/dot_general | solution.py:79
  (89 shorter events, 11.6 us)
Async XLA Ops:
  6.5 6.1 %copy-start.3 = (s32[64]{0:T(128)S(1)}, s32[64]{0:T(128)}, u32[]{:S(2)}) copy-start(s32[64]{0:T(128)} %param.11) | copy-start | bytes 772
  6.5 6.1 %copy-start.4 = (s32[64]{0:T(128)S(1)}, s32[64]{0:T(128)}, u32[]{:S(2)}) copy-start(s32[64]{0:T(128)} %param.12) | copy-start | bytes 772
  6.5 291.3 %all-gather.3.cloned.1.call-start = ((), (), s32[]{:S(2)}) async-start(), calls=%async_computation.1 | async-start | bytes 4325376 | tf_op jit(solution)/shard_map/all_gather | solution.py:70
  12.6 20.5 %copy-start.5 = (u32[256]{0:T(256)S(1)}, u32[256]{0:T(256)}, u32[]{:S(2)}) copy-start(u32[256]{0:T(256)} %constant.149) | copy-start | bytes 3076
  17.7 135.5 %all-to-all-start = ((f32[256,1,2,8,128]{4,3,2,1,0:T(8,128)}), f32[256,1,2,8,128]{4,3,2,1,0:T(8,128)S(1)}, u32[]{:S(2)}, u32[]{:S(2)}) async-start(f32[256,1,2,8,128]{4,3,2,1,0:T(8,128)} %stack.15), calls=%async_computation | async-start | bytes 4194304 | tf_op jit(solution)/shard_map/all_to_all | solution.py:31
  32.3 330.0 %all-gather.5.cloned.1.call-start = ((), (), s32[]{:S(2)}) async-start(), calls=%async_computation.2 | async-start | bytes 4325376 | tf_op jit(solution)/shard_map/all_gather | solution.py:72
  230.9 66.9 %copy-start.1 = (bf16[256,4096]{1,0:T(8,128)(2,1)S(1)}, bf16[256,4096]{1,0:T(8,128)(2,1)}, u32[]{:S(2)}) copy-start(bf16[256,4096]{1,0:T(8,128)(2,1)} %param.8) | copy-start | bytes 6291460
  231.7 0.7 copy-start.2
  362.4 8.0 %copy-start = (f32[256,4096]{1,0:T(8,128)S(1)}, f32[256,4096]{1,0:T(8,128)}, u32[]{:S(2)}) copy-start(f32[256,4096]{1,0:T(8,128)} %convolution_subtract_fusion.2) | copy-start | bytes 12582916
Sparse Core Ops, SparseCore 0:
  9.2 93.4 all-gather.2
  104.6 61.7 all-gather.4
